TPU v7x, 128 devices: a whole 4x4x4 slice. The times are simulated.
128 devices in a mesh: row: 4 (over y_lo, core), col: 32 (over y_hi, z, x).
Axes of the slice: x: 4, y: 4 (y_hi: 2, y_lo: 2; y = y_hi * 2 + y_lo), z: 4, core: 2. Of those that a mesh axis runs over, the one named last changes fastest.
Arguments:
- sky: bfloat16 [128, 1024, 4096], P(None, 'row', 'col'), may hold values from -80 to 80
- kernel_widths: int32 [2], replicated, may hold values from 16 to 32, as said below
- prior_var: float32 [2, 128], replicated, may hold values from 0.05 to 0.5
- tile_region: int32 [4, 32], P('row', 'col'), may hold values from 0 to 7, as said below
- region_rank: int32 [8], replicated, may hold values from 2 to 8
Outputs:
- cleaned: bfloat16 [128, 1024, 4096], P(None, 'row', 'col')
Inputs may be any that keep to these rules, and one draw needn't show every extreme that they name: `kernel_widths`: entry 0 is the half-width along the sky's rows (second dimension of sky), entry 1 along its columns; one of the two equals 32, the other is below 32. `tile_region`: each region holds exactly 16 tiles, anywhere on the sky.
All inputs are finite; a program needn't handle non-finite values.
Results may differ from a plain program's by a relative error of at most 0.0085.
Values may be sent and summed in bfloat16 or wider, within the bound.
A program may use at most 128 MiB of HBM per device.

v0:
```python
import math
import jax
import jax.numpy as jnp
from jax import lax
from jax.sharding import PartitionSpec as P

HW = 32
MMAX = 8
TPR = 16


def extended_2(cells, sides, width):
    for axis, dim in sides:
        count = lax.axis_size(axis)
        ends = count - 1
        head = lax.slice_in_dim(cells, 0, width, axis=dim)
        tail = lax.slice_in_dim(cells, cells.shape[dim] - width, cells.shape[dim], axis=dim)
        cells = jnp.concatenate(
            [
                lax.ppermute(tail, axis, [(i, (i + 1) % count) for i in range(ends)]),
                cells,
                lax.ppermute(head, axis, [((i + 1) % count, i) for i in range(ends)]),
            ],
            axis=dim,
        )
    return cells


def raised(offsets, half_width):
    spread = half_width.astype(jnp.float32)
    inside = jnp.abs(offsets) <= spread
    values = (1.0 + jnp.cos(math.pi * offsets / (spread + 1.0))) / (2.0 * spread + 2.0)
    return jnp.where(inside, values, jnp.zeros_like(values))


def toeplitz(length, half_width):
    inputs = jnp.arange(length + 2 * HW, dtype=jnp.float32)[:, None]
    outputs = jnp.arange(length, dtype=jnp.float32)[None, :]
    offsets = inputs - outputs - HW
    return raised(offsets, half_width).astype(jnp.bfloat16)


def chebyshev(chan_count, degree):
    position = (2.0 * jnp.arange(chan_count, dtype=jnp.float32) + 1.0) / chan_count - 1.0
    terms = [jnp.ones_like(position), position]
    for order in range(2, degree):
        terms.append(2.0 * position * terms[-1] - terms[-2])
    return jnp.stack(terms[:degree], axis=1)


def spd_solve(matrix, right_hand):
    factor = jnp.linalg.cholesky(matrix)
    middle = lax.linalg.triangular_solve(factor, right_hand, left_side=True, lower=True)
    return lax.linalg.triangular_solve(factor, middle, left_side=True, lower=True, transpose_a=True)


def projector(gram_sum, prior_row, keep_rank, pixels):
    chan_count = gram_sum.shape[0]
    cheb_basis = chebyshev(chan_count, MMAX)
    covariance = gram_sum / pixels + jnp.diag(prior_row)
    mixed = spd_solve(covariance, cheb_basis)
    keep_mask = (jnp.arange(MMAX) < keep_rank).astype(jnp.float32)
    kept_basis = cheb_basis * keep_mask
    kept_mixed = mixed * keep_mask
    small_matrix = jnp.dot(kept_basis.T, kept_mixed, precision=lax.Precision.HIGHEST) + jnp.diag(
        1.0 - keep_mask
    )
    weights = spd_solve(small_matrix, kept_mixed.T)
    return jnp.dot(kept_basis, weights, precision=lax.Precision.HIGHEST).astype(jnp.bfloat16)


def local(sky, kernel_widths, prior_var, tile_region, region_rank):
    chan_count, tile_rows, tile_cols = sky.shape
    down_table = toeplitz(tile_rows, kernel_widths[0])
    across_table = toeplitz(tile_cols, kernel_widths[1])
    extended = extended_2(sky, (("row", 1), ("col", 2)), HW)
    smooth = jnp.einsum(
        "cyx,yz->czx", extended, down_table, preferred_element_type=jnp.float32
    ).astype(jnp.bfloat16)
    coarse = jnp.einsum(
        "cyx,xz->cyz", smooth, across_table, preferred_element_type=jnp.float32
    ).astype(jnp.bfloat16)
    fine = (sky.astype(jnp.float32) - coarse.astype(jnp.float32)).astype(jnp.bfloat16)
    coarse_gram = jnp.einsum("cyx,dyx->cd", coarse, coarse, preferred_element_type=jnp.float32)
    fine_gram = jnp.einsum("cyx,dyx->cd", fine, fine, preferred_element_type=jnp.float32)
    grams = jnp.stack([coarse_gram, fine_gram], axis=0)
    region = tile_region[0, 0]
    region_count = region_rank.shape[0]
    slot_mask = (jnp.arange(region_count) == region).astype(jnp.float32)
    slotted = slot_mask[:, None, None, None] * grams[None]
    totals = lax.psum(slotted, ("row", "col"))
    own_gram = lax.dynamic_index_in_dim(totals, region, 0, keepdims=False)
    keep_rank = lax.dynamic_index_in_dim(region_rank, region, 0, keepdims=False)
    pixels = TPR * tile_rows * tile_cols
    coarse_proj = projector(own_gram[0], prior_var[0], keep_rank, pixels)
    fine_proj = projector(own_gram[1], prior_var[1], keep_rank, pixels)
    removed = jnp.einsum("ij,jyx->iyx", coarse_proj, coarse, preferred_element_type=jnp.float32)
    removed = removed + jnp.einsum(
        "ij,jyx->iyx", fine_proj, fine, preferred_element_type=jnp.float32
    )
    cleaned = coarse.astype(jnp.float32) + fine.astype(jnp.float32) - removed
    return cleaned.astype(jnp.bfloat16)


def solution(mesh):
    return jax.shard_map(
        local,
        mesh=mesh,
        in_specs=(P(None, "row", "col"), P(), P(), P("row", "col"), P()),
        out_specs=P(None, "row", "col"),
        check_vma=False,
    )
```

profile of v0, /device:TPU:1, one launch (start us, length us, event | category | flops | bytes accessed | tf_op | source)
XLA Modules:
  0.0 505.3 jit_solution(14698396365791912761)
XLA Ops:
  6.5 12.7 %copy.25 = bf16[128,256,128]{0,2,1:T(8,128)(2,1)} copy(bf16[128,256,128]{2,1,0:T(8,128)(2,1)} %param.15) | data formatting | bytes 16777216 | tf_op args[0]
  19.2 1.7 fusion.87
  20.9 4.6 collective-permute-start
  25.5 1.9 collective-permute-start.1
  27.4 9.8 %collective-permute-done = bf16[128,32,128]{0,2,1:T(8,128)(2,1)S(1)} collective-permute-done((bf16[128,32,128]{0,2,1:T(8,128)(2,1)S(1)}, bf16[128,32,128]{0,2,1:T(8,128)(2,1)S(1)}, u32[]{:S(2)}, u32[]{:S(2)}) %collective-permute-start) | collective-permute-done | bytes 1048608 | tf_op jit(solution)/shard_map/ppermute | solution.py:20
  37.2 4.4 collective-permute-done.1
  41.6 7.7 %pad_maximum_fusion.3 = (bf16[128,320,32]{0,2,1:T(8,128)(2,1)}, bf16[128,320,32]{0,2,1:T(8,128)(2,1)}) fusion(bf16[128,32,128]{0,2,1:T(8,128)(2,1)S(1)} %collective-permute-done.1, bf16[128,256,128]{0,2,1:T(8,128)(2,1)} %copy.25, bf16[128,32,128]{0,2,1:T(8,128)(2,1)S(1)} %collective-permute-done), kind=kLoop, calls=%fused_computation.18 | loop fusion | flops 15728640 | bytes 15728640 | tf_op jit(solution)/shard_map/slice | solution.py:17
  49.3 4.6 collective-permute-start.2
  53.9 1.5 collective-permute-start.3
  55.4 0.6 fusion.88
  58.0 0.6 dynamic_slice.8
  58.7 39.6 %collective-permute-done.2 = bf16[128,320,32]{0,2,1:T(8,128)(2,1)} collective-permute-done((bf16[128,320,32]{0,2,1:T(8,128)(2,1)}, bf16[128,320,32]{0,2,1:T(8,128)(2,1)}, u32[]{:S(2)}, u32[]{:S(2)}) %collective-permute-start.2) | collective-permute-done | bytes 2621472 | tf_op jit(solution)/shard_map/ppermute | solution.py:20
  98.3 5.6 %collective-permute-done.3 = bf16[128,320,32]{0,2,1:T(8,128)(2,1)} collective-permute-done((bf16[128,320,32]{0,2,1:T(8,128)(2,1)}, bf16[128,320,32]{0,2,1:T(8,128)(2,1)}, u32[]{:S(2)}, u32[]{:S(2)}) %collective-permute-start.3) | collective-permute-done | bytes 2621472 | tf_op jit(solution)/shard_map/ppermute | solution.py:22
  103.9 29.0 %pad_maximum_fusion = bf16[128,320,192]{0,2,1:T(8,128)(2,1)} fusion(bf16[128,320,32]{0,2,1:T(8,128)(2,1)} %collective-permute-done.3, bf16[128,32,128]{0,2,1:T(8,128)(2,1)S(1)} %collective-permute-done.1, bf16[128,256,128]{0,2,1:T(8,128)(2,1)} %copy.25, bf16[128,32,128]{0,2,1:T(8,128)(2,1)S(1)} %collective-permute-done, ...), kind=kLoop, calls=%fused_computation.6 | loop fusion | flops 78643200 | bytes 31457280 | tf_op jit(solution)/shard_map/concatenate | solution.py:18
  133.0 26.4 %copy.47 = bf16[128,320,192]{1,2,0:T(8,128)(2,1)} copy(bf16[128,320,192]{0,2,1:T(8,128)(2,1)} %pad_maximum_fusion) | data formatting | bytes 31457280 | tf_op jit(solution)/shard_map/concatenate | solution.py:18
  159.3 25.8 %fusion = (bf16[128,256,128]{2,1,0:T(8,128)(2,1)}, bf16[128,256,128]{2,1,0:T(8,128)(2,1)}) fusion(bf16[128,256,128]{2,1,0:T(8,128)(2,1)} %param.15, f32[]{:T(128)S(6)} %add.184, f32[]{:T(128)S(6)} %add.181, f32[]{:T(128)} %bitcast.4, bf16[128,320,192]{1,2,0:T(8,128)(2,1)} %copy.47, f32[]{:T(128)S(6)} %add.180, f32[]{:T(128)S(6)} %add.177, f32[]{:T(128)} %bitcast.1), kind=kOutput, calls=%fused_computation.2 | convolution fusion | flops 5665472512 | bytes 40894488 | tf_op jit(solution)/shard_map/cyx,xz->cyz/dot_general | solution.py:80
  185.1 12.5 %copy.30 = bf16[128,256,128]{1,0,2:T(8,128)(2,1)} copy(bf16[128,256,128]{2,1,0:T(8,128)(2,1)} %get-tuple-element.21) | data formatting | bytes 16777216 | tf_op jit(solution)/shard_map/convert_element_type | solution.py:83
  197.7 8.1 %convolution_bitcast_fusion = f32[1,128,128]{2,1,0:T(8,128)S(1)} fusion(bf16[128,256,128]{1,0,2:T(8,128)(2,1)} %copy.30), kind=kOutput, calls=%fused_computation.19 | convolution fusion | flops 1073741824 | bytes 8454144 | tf_op jit(solution)/shard_map/cyx,dyx->cd/dot_general | solution.py:85
  205.8 12.9 %copy.28 = bf16[128,256,128]{1,0,2:T(8,128)(2,1)} copy(bf16[128,256,128]{2,1,0:T(8,128)(2,1)} %get-tuple-element.22) | data formatting | bytes 16777216 | tf_op jit(solution)/shard_map/convert_element_type | solution.py:82
  218.7 8.1 %convolution_bitcast_fusion.1 = f32[1,128,128]{2,1,0:T(8,128)S(1)} fusion(bf16[128,256,128]{1,0,2:T(8,128)(2,1)} %copy.28), kind=kOutput, calls=%fused_computation.20 | convolution fusion | flops 1073741824 | bytes 8454144 | tf_op jit(solution)/shard_map/cyx,dyx->cd/dot_general | solution.py:84
  226.8 0.1 copy.32
  226.9 1.2 broadcast_multiply_fusion
  228.1 0.0 all-reduce.2.cloned.1.call-update
  228.2 0.6 compare_convert_fusion.1
  228.8 0.6 broadcast_subtract_fusion
  229.5 150.2 %all-reduce.2.cloned.1.call-done = f32[8,2,128,128]{2,3,1,0:T(8,128)} async-done(((f32[8,2,128,128]{2,3,1,0:T(8,128)}), f32[8,2,128,128]{2,3,1,0:T(8,128)}) %all-reduce.2.cloned.1.call-update) | async-done | bytes 1048592 | tf_op jit(solution)/shard_map/psum | solution.py:91
  379.7 0.9 fusion.39
  380.6 0.1 copy.33
  380.7 0.1 copy.39
  380.9 11.7 %cholesky.108 = f32[128,128]{1,0:T(8,128)S(1)} custom-call(f32[128,128]{1,0:T(8,128)S(1)} %get-tuple-element.29), custom_call_target="Cholesky" | custom-call | tf_op jit(solution)/shard_map/jit(cholesky)/cholesky | solution.py:52
  392.6 0.7 compare_reduce_fusion.1
  393.3 0.6 fusion.35
  393.9 9.8 %custom-call.25 = f32[1,128,128]{1,2,0:T(8,128)S(1)} custom-call(f32[1,128,128]{2,1,0:T(8,128)S(1)} %fusion.35), custom_call_target="InvertDiagBlocksLowerTriangular" | custom-call | tf_op jit(solution)/shard_map/triangular_solve/custom-call.3 | solution.py:54
  403.7 11.7 %cholesky.86 = f32[128,128]{1,0:T(8,128)S(1)} custom-call(f32[128,128]{1,0:T(8,128)S(1)} %get-tuple-element.30), custom_call_target="Cholesky" | custom-call | tf_op jit(solution)/shard_map/jit(cholesky)/cholesky | solution.py:52
  415.5 0.7 compare_reduce_fusion.3
  416.2 0.6 fusion.34
  416.8 10.0 %custom-call.21 = f32[1,128,128]{1,2,0:T(8,128)S(1)} custom-call(f32[1,128,128]{2,1,0:T(8,128)S(1)} %fusion.34), custom_call_target="InvertDiagBlocksLowerTriangular" | custom-call | tf_op jit(solution)/shard_map/triangular_solve/custom-call.3 | solution.py:54
  426.8 0.3 fusion.44
  427.1 0.2 convolution_multiply_fusion.1
  427.2 0.3 convolution_add_fusion.1
  427.5 0.1 copy.35
  427.6 0.7 cholesky.97
  428.3 0.1 select_reduce_fusion.3
  428.4 0.7 compare_reduce_fusion.2
  429.0 0.6 fusion.57
  429.7 0.6 custom-call.23
  430.3 0.2 fusion.63
  430.5 0.1 fusion.65
  430.6 0.4 fusion.15
  431.0 0.3 fusion.40
  431.3 0.2 convolution_multiply_fusion
  431.5 0.3 convolution_add_fusion
  431.7 0.1 copy.41
  431.8 0.7 cholesky.119
  432.5 0.1 select_reduce_fusion.2
  432.6 0.7 compare_reduce_fusion
  433.3 0.6 fusion.58
  433.9 0.6 custom-call.27
  434.5 0.2 fusion.59
  434.7 0.1 fusion.61
  434.9 0.4 fusion.16
  435.3 15.6 %fusion.8 = f32[128,256,128]{2,0,1:T(8,128)} fusion(bf16[128,128,1]{1,0,2:T(8,128)(2,1)S(1)} %fusion.16, bf16[128,256,128]{2,1,0:T(8,128)(2,1)} %get-tuple-element.21), kind=kOutput, calls=%fused_computation.11 | convolution fusion | flops 1073741824 | bytes 25198592 | tf_op jit(solution)/shard_map/ij,jyx->iyx/dot_general | solution.py:98
  450.8 15.8 %fusion.10 = f32[128,256,128]{2,0,1:T(8,128)} fusion(bf16[128,128,1]{1,0,2:T(8,128)(2,1)S(1)} %fusion.15, bf16[128,256,128]{2,1,0:T(8,128)(2,1)} %get-tuple-element.22), kind=kOutput, calls=%fused_computation.13 | convolution fusion | flops 1073741824 | bytes 25198592 | tf_op jit(solution)/shard_map/ij,jyx->iyx/dot_general | solution.py:97
  466.6 31.6 %fusion.2 = bf16[128,256,128]{2,1,0:T(8,128)(2,1)} fusion(bf16[128,256,128]{2,1,0:T(8,128)(2,1)S(1)} %bitcast.129, f32[128,256,128]{2,0,1:T(8,128)} %fusion.8, f32[128,256,128]{2,0,1:T(8,128)} %fusion.10, bf16[128,256,128]{2,1,0:T(8,128)(2,1)S(1)} %bitcast.131), kind=kLoop, calls=%fused_computation.4 | loop fusion | flops 37748736 | bytes 58720256 | tf_op jit(solution)/shard_map/convert_element_type | solution.py:102
  (31 shorter events, 0.3 us)
Async XLA Ops:
  6.5 373.2 %all-reduce.2.cloned.1.call-start = ((), (), s32[]{:S(2)}) async-start(), calls=%async_computation | async-start | bytes 2097152 | tf_op jit(solution)/shard_map/psum | solution.py:91
  20.9 34.5 %copy-start = (s32[2]{0:T(128)S(1)}, s32[2]{0:T(128)}, u32[]{:S(2)}) copy-start(s32[2]{0:T(128)} %param.16) | copy-start | bytes 28
  20.9 37.1 %copy-start.2 = (s32[8]{0:T(128)S(1)}, s32[8]{0:T(128)}, u32[]{:S(2)}) copy-start(s32[8]{0:T(128)} %param.19) | copy-start | bytes 100
  20.9 16.3 %collective-permute-start = (bf16[128,32,128]{0,2,1:T(8,128)(2,1)S(1)}, bf16[128,32,128]{0,2,1:T(8,128)(2,1)S(1)}, u32[]{:S(2)}, u32[]{:S(2)}) collective-permute-start(bf16[128,32,128]{0,2,1:T(8,128)(2,1)S(1)} %get-tuple-element.10), channel_id=1, source_target_pairs={{0,32},{32,64},{64,96},{1,33},{33,65},{65,97},{2,34},{34,66},{66,9... | collective-permute-start | bytes 3145736 | tf_op jit(solution)/shard_map/ppermute | solution.py:20
  25.5 16.1 %collective-permute-start.1 = (bf16[128,32,128]{0,2,1:T(8,128)(2,1)S(1)}, bf16[128,32,128]{0,2,1:T(8,128)(2,1)S(1)}, u32[]{:S(2)}, u32[]{:S(2)}) collective-permute-start(bf16[128,32,128]{0,2,1:T(8,128)(2,1)S(1)} %get-tuple-element.12), channel_id=1, source_target_pairs={{32,0},{64,32},{96,64},{33,1},{65,33},{97,65},{34,2},{66,34},{98,6... | collective-permute-start | bytes 3145736 | tf_op jit(solution)/shard_map/ppermute | solution.py:22
  49.3 49.0 %collective-permute-start.2 = (bf16[128,320,32]{0,2,1:T(8,128)(2,1)}, bf16[128,320,32]{0,2,1:T(8,128)(2,1)}, u32[]{:S(2)}, u32[]{:S(2)}) collective-permute-start(bf16[128,320,32]{0,2,1:T(8,128)(2,1)} %get-tuple-element.6), channel_id=1, source_target_pairs={{0,1},{1,2},{2,3},{3,4},{4,5},{5,6},{6,7},{7,8},{8,9},{9,10},{10,1... | collective-permute-start | bytes 7864328 | tf_op jit(solution)/shard_map/ppermute | solution.py:20
  53.9 50.0 %collective-permute-start.3 = (bf16[128,320,32]{0,2,1:T(8,128)(2,1)}, bf16[128,320,32]{0,2,1:T(8,128)(2,1)}, u32[]{:S(2)}, u32[]{:S(2)}) collective-permute-start(bf16[128,320,32]{0,2,1:T(8,128)(2,1)} %get-tuple-element.8), channel_id=1, source_target_pairs={{1,0},{2,1},{3,2},{4,3},{5,4},{6,5},{7,6},{8,7},{9,8},{10,9},{11,1... | collective-permute-start | bytes 7864328 | tf_op jit(solution)/shard_map/ppermute | solution.py:22
  218.7 10.8 %copy-start.1 = (f32[2,128]{1,0:T(2,128)S(1)}, f32[2,128]{1,0:T(2,128)}, u32[]{:S(2)}) copy-start(f32[2,128]{1,0:T(2,128)} %param.17) | copy-start | bytes 3076
  435.2 31.4 %slice-start = ((s8[8388608]{0:T(1024)(128)(4,1)}), s8[4194304]{0:T(1024)(128)(4,1)S(1)}, s32[]{:S(2)}) async-start(s8[8388608]{0:T(1024)(128)(4,1)} %bitcast.128), calls=%async_computation.1 | async-start | bytes 8388608
  435.2 31.4 %slice-start.2 = ((s8[8388608]{0:T(1024)(128)(4,1)}), s8[4194304]{0:T(1024)(128)(4,1)S(1)}, s32[]{:S(2)}) async-start(s8[8388608]{0:T(1024)(128)(4,1)} %bitcast.130), calls=%async_computation.3 | async-start | bytes 8388608
  450.8 15.8 %slice-start.1 = ((s8[8388608]{0:T(1024)(128)(4,1)}), s8[4194304]{0:T(1024)(128)(4,1)S(1)}, s32[]{:S(2)}) async-start(s8[8388608]{0:T(1024)(128)(4,1)} %bitcast.128), calls=%async_computation.2 | async-start | bytes 8388608
  450.8 15.8 %slice-start.3 = ((s8[8388608]{0:T(1024)(128)(4,1)}), s8[4194304]{0:T(1024)(128)(4,1)S(1)}, s32[]{:S(2)}) async-start(s8[8388608]{0:T(1024)(128)(4,1)} %bitcast.130), calls=%async_computation.4 | async-start | bytes 8388608
Sparse Core Ops, SparseCore 0:
  228.3 151.4 all-reduce.1
where the time goes:
time: 510 us; the launch traced here: 505 us
  waiting for transfers between devices  210 us (41%)
  other arithmetic  123 us (24%)
  matrix products  76.2 us (15%)
  local copies, waits for them, and re-layouts  68 us (13%)
  between operations  15.9 us (3%)
  starting transfers between devices  12.6 us (2%)
    psum x1, waiting for transfers between devices, local(): totals = lax.psum(slotted, ('row', 'col'))  150 us
    ppermute x2, waiting for transfers between devices, extended_2(): lax.ppermute(tail, axis, [(i, (i + 1) % count) for i in range(ends)])  49.4 us
    convert_element_type x1, other arithmetic, local(): return cleaned.astype(jnp.bfloat16)  31.6 us
    concatenate x1, other arithmetic, extended_2(): jnp.concatenate([lax.ppermute(tail, axis, [(i, (i + 1) % count) for i in...  29 us
    another operation x12, other arithmetic, spd_solve(): factor = jnp.linalg.cholesky(matrix)  27.7 us
    concatenate x1, local copies, waits for them, and re-layouts, extended_2(): jnp.concatenate([lax.ppermute(tail, axis, [(i, (i + 1) % count) for i in...  26.4 us
    dot_general x1, matrix products, local(): jnp.einsum('cyx,xz->cyz', smooth, across_table, preferred_element_type=jn...  25.8 us
    another operation x8, other arithmetic, spd_solve(): lax.linalg.triangular_solve(factor, middle, left_side=True, lower=True, t...  23.6 us
  transfers between devices with their start and end apart: 5, of which 5 were waited for; matrix products, arithmetic and copies ran while one was open for 1% of the time, Pallas kernels for 0%

commit v1 on v0

--- a/solution.py
+++ b/solution.py
@@ -88,7 +88,7 @@
     region_count = region_rank.shape[0]
     slot_mask = (jnp.arange(region_count) == region).astype(jnp.float32)
     slotted = slot_mask[:, None, None, None] * grams[None]
-    totals = lax.psum(slotted, ("row", "col"))
+    totals = lax.psum(lax.psum(slotted, "col"), "row")
     own_gram = lax.dynamic_index_in_dim(totals, region, 0, keepdims=False)
     keep_rank = lax.dynamic_index_in_dim(region_rank, region, 0, keepdims=False)
     pixels = TPR * tile_rows * tile_cols

time: 510 us -> 761 us (1.49)
  waiting for transfers between devices: 210 us -> 460 us
    psum x1 -> x2, waiting for transfers between devices: 150 us -> 401 us  [local(): totals = lax.psum(lax.psum(slotted, 'col'), 'row')]
  transfers between devices with their start and end apart: 5 -> 6, of which waited for: 5 -> 6; matrix products, arithmetic and copies ran while one was open for 1% -> 0% of each run, Pallas kernels for 0% -> 0%
where the time goes in v1:
time: 761 us; the launch traced here: 756 us
  waiting for transfers between devices  460 us (60%)
  other arithmetic  123 us (16%)
  matrix products  76.2 us (10%)
  local copies, waits for them, and re-layouts  67.7 us (9%)
  between operations  16.1 us (2%)
  starting transfers between devices  13 us (2%)
    psum x2, waiting for transfers between devices, local(): totals = lax.psum(lax.psum(slotted, 'col'), 'row')  401 us
    ppermute x2, waiting for transfers between devices, extended_2(): lax.ppermute(tail, axis, [(i, (i + 1) % count) for i in range(ends)])  49.7 us
    convert_element_type x1, other arithmetic, local(): return cleaned.astype(jnp.bfloat16)  31.6 us
    concatenate x1, other arithmetic, extended_2(): jnp.concatenate([lax.ppermute(tail, axis, [(i, (i + 1) % count) for i in...  29 us
    another operation x12, other arithmetic, spd_solve(): factor = jnp.linalg.cholesky(matrix)  27.7 us
    concatenate x1, local copies, waits for them, and re-layouts, extended_2(): jnp.concatenate([lax.ppermute(tail, axis, [(i, (i + 1) % count) for i in...  26.4 us
    dot_general x1, matrix products, local(): jnp.einsum('cyx,xz->cyz', smooth, across_table, preferred_element_type=jn...  25.8 us
    another operation x8, other arithmetic, spd_solve(): lax.linalg.triangular_solve(factor, middle, left_side=True, lower=True, t...  23.6 us
  transfers between devices with their start and end apart: 6, of which 6 were waited for; matrix products, arithmetic and copies ran while one was open for 0% of the time, Pallas kernels for 0%

profile of v1, /device:TPU:1, one launch (start us, length us, event | category | flops | bytes accessed | tf_op | source)
XLA Modules:
  0.0 756.5 jit_solution(10722234215328519609)
XLA Ops:
  6.5 12.7 %copy.25 = bf16[128,256,128]{0,2,1:T(8,128)(2,1)} copy(bf16[128,256,128]{2,1,0:T(8,128)(2,1)} %param.15) | data formatting | bytes 16777216 | tf_op args[0]
  19.2 1.7 fusion.87
  20.9 4.6 collective-permute-start
  25.5 1.9 collective-permute-start.1
  27.4 9.8 %collective-permute-done = bf16[128,32,128]{0,2,1:T(8,128)(2,1)S(1)} collective-permute-done((bf16[128,32,128]{0,2,1:T(8,128)(2,1)S(1)}, bf16[128,32,128]{0,2,1:T(8,128)(2,1)S(1)}, u32[]{:S(2)}, u32[]{:S(2)}) %collective-permute-start) | collective-permute-done | bytes 1048608 | tf_op jit(solution)/shard_map/ppermute | solution.py:20
  37.2 4.4 collective-permute-done.1
  41.6 7.7 %pad_maximum_fusion.3 = (bf16[128,320,32]{0,2,1:T(8,128)(2,1)}, bf16[128,320,32]{0,2,1:T(8,128)(2,1)}) fusion(bf16[128,32,128]{0,2,1:T(8,128)(2,1)S(1)} %collective-permute-done.1, bf16[128,256,128]{0,2,1:T(8,128)(2,1)} %copy.25, bf16[128,32,128]{0,2,1:T(8,128)(2,1)S(1)} %collective-permute-done), kind=kLoop, calls=%fused_computation.18 | loop fusion | flops 15728640 | bytes 15728640 | tf_op jit(solution)/shard_map/slice | solution.py:17
  49.3 4.6 collective-permute-start.2
  53.9 1.8 collective-permute-start.3
  55.8 0.6 fusion.88
  58.4 40.0 %collective-permute-done.2 = bf16[128,320,32]{0,2,1:T(8,128)(2,1)} collective-permute-done((bf16[128,320,32]{0,2,1:T(8,128)(2,1)}, bf16[128,320,32]{0,2,1:T(8,128)(2,1)}, u32[]{:S(2)}, u32[]{:S(2)}) %collective-permute-start.2) | collective-permute-done | bytes 2621472 | tf_op jit(solution)/shard_map/ppermute | solution.py:20
  98.3 5.6 collective-permute-done.3
  103.9 29.0 %pad_maximum_fusion = bf16[128,320,192]{0,2,1:T(8,128)(2,1)} fusion(bf16[128,320,32]{0,2,1:T(8,128)(2,1)} %collective-permute-done.3, bf16[128,32,128]{0,2,1:T(8,128)(2,1)S(1)} %collective-permute-done.1, bf16[128,256,128]{0,2,1:T(8,128)(2,1)} %copy.25, bf16[128,32,128]{0,2,1:T(8,128)(2,1)S(1)} %collective-permute-done, ...), kind=kLoop, calls=%fused_computation.6 | loop fusion | flops 78643200 | bytes 31457280 | tf_op jit(solution)/shard_map/concatenate | solution.py:18
  132.9 26.4 %copy.47 = bf16[128,320,192]{1,2,0:T(8,128)(2,1)} copy(bf16[128,320,192]{0,2,1:T(8,128)(2,1)} %pad_maximum_fusion) | data formatting | bytes 31457280 | tf_op jit(solution)/shard_map/concatenate | solution.py:18
  159.3 25.8 %fusion = (bf16[128,256,128]{2,1,0:T(8,128)(2,1)}, bf16[128,256,128]{2,1,0:T(8,128)(2,1)}) fusion(bf16[128,256,128]{2,1,0:T(8,128)(2,1)} %param.15, f32[]{:T(128)S(6)} %add.186, f32[]{:T(128)S(6)} %add.183, f32[]{:T(128)} %bitcast.4, bf16[128,320,192]{1,2,0:T(8,128)(2,1)} %copy.47, f32[]{:T(128)S(6)} %add.182, f32[]{:T(128)S(6)} %add.179, f32[]{:T(128)} %bitcast.1), kind=kOutput, calls=%fused_computation.2 | convolution fusion | flops 5665472512 | bytes 40894488 | tf_op jit(solution)/shard_map/cyx,xz->cyz/dot_general | solution.py:80
  185.1 12.7 %copy.30 = bf16[128,256,128]{1,0,2:T(8,128)(2,1)} copy(bf16[128,256,128]{2,1,0:T(8,128)(2,1)} %get-tuple-element.21) | data formatting | bytes 16777216 | tf_op jit(solution)/shard_map/convert_element_type | solution.py:83
  197.8 8.1 %convolution_bitcast_fusion = f32[1,128,128]{2,1,0:T(8,128)S(1)} fusion(bf16[128,256,128]{1,0,2:T(8,128)(2,1)} %copy.30), kind=kOutput, calls=%fused_computation.19 | convolution fusion | flops 1073741824 | bytes 8454144 | tf_op jit(solution)/shard_map/cyx,dyx->cd/dot_general | solution.py:85
  205.9 12.6 %copy.28 = bf16[128,256,128]{1,0,2:T(8,128)(2,1)} copy(bf16[128,256,128]{2,1,0:T(8,128)(2,1)} %get-tuple-element.22) | data formatting | bytes 16777216 | tf_op jit(solution)/shard_map/convert_element_type | solution.py:82
  218.5 8.1 %convolution_bitcast_fusion.1 = f32[1,128,128]{2,1,0:T(8,128)S(1)} fusion(bf16[128,256,128]{1,0,2:T(8,128)(2,1)} %copy.28), kind=kOutput, calls=%fused_computation.20 | convolution fusion | flops 1073741824 | bytes 8454144 | tf_op jit(solution)/shard_map/cyx,dyx->cd/dot_general | solution.py:84
  226.6 0.1 copy.32
  226.7 1.2 broadcast_multiply_fusion
  228.0 337.1 %all-reduce.3.cloned.1.call-done = f32[8,2,128,128]{2,3,1,0:T(8,128)} async-done(((f32[8,2,128,128]{2,3,1,0:T(8,128)}), f32[8,2,128,128]{2,3,1,0:T(8,128)}) %all-reduce.3.cloned.1.call-update) | async-done | bytes 1048592 | tf_op jit(solution)/shard_map/psum | solution.py:91
  565.1 0.6 dynamic_slice.8
  565.8 0.6 compare_convert_fusion.1
  566.5 0.6 broadcast_subtract_fusion
  567.1 63.5 %all-reduce.5.cloned.1.call-done = f32[8,2,128,128]{2,3,1,0:T(8,128)} async-done(((f32[8,2,128,128]{2,3,1,0:T(8,128)}), f32[8,2,128,128]{2,3,1,0:T(8,128)}) %all-reduce.5.cloned.1.call-update) | async-done | bytes 1048592 | tf_op jit(solution)/shard_map/psum | solution.py:91
  630.6 0.9 fusion.39
  631.5 0.1 copy.33
  631.6 0.1 copy.39
  631.8 11.7 %cholesky.108 = f32[128,128]{1,0:T(8,128)S(1)} custom-call(f32[128,128]{1,0:T(8,128)S(1)} %get-tuple-element.29), custom_call_target="Cholesky" | custom-call | tf_op jit(solution)/shard_map/jit(cholesky)/cholesky | solution.py:52
  643.5 0.7 compare_reduce_fusion.1
  644.2 0.6 fusion.35
  644.8 9.8 %custom-call.25 = f32[1,128,128]{1,2,0:T(8,128)S(1)} custom-call(f32[1,128,128]{2,1,0:T(8,128)S(1)} %fusion.35), custom_call_target="InvertDiagBlocksLowerTriangular" | custom-call | tf_op jit(solution)/shard_map/triangular_solve/custom-call.3 | solution.py:54
  654.6 11.7 %cholesky.86 = f32[128,128]{1,0:T(8,128)S(1)} custom-call(f32[128,128]{1,0:T(8,128)S(1)} %get-tuple-element.30), custom_call_target="Cholesky" | custom-call | tf_op jit(solution)/shard_map/jit(cholesky)/cholesky | solution.py:52
  666.4 0.7 compare_reduce_fusion.3
  667.1 0.6 fusion.34
  667.7 10.0 %custom-call.21 = f32[1,128,128]{1,2,0:T(8,128)S(1)} custom-call(f32[1,128,128]{2,1,0:T(8,128)S(1)} %fusion.34), custom_call_target="InvertDiagBlocksLowerTriangular" | custom-call | tf_op jit(solution)/shard_map/triangular_solve/custom-call.3 | solution.py:54
  677.7 0.3 fusion.44
  678.0 0.2 convolution_multiply_fusion.1
  678.2 0.3 convolution_add_fusion.1
  678.4 0.1 copy.35
  678.5 0.7 cholesky.97
  679.2 0.1 select_reduce_fusion.3
  679.3 0.7 compare_reduce_fusion.2
  680.0 0.6 fusion.57
  680.6 0.6 custom-call.23
  681.2 0.2 fusion.63
  681.4 0.1 fusion.65
  681.6 0.4 fusion.15
  681.9 0.3 fusion.40
  682.2 0.2 convolution_multiply_fusion
  682.4 0.3 convolution_add_fusion
  682.7 0.1 copy.41
  682.8 0.7 cholesky.119
  683.5 0.1 select_reduce_fusion.2
  683.5 0.7 compare_reduce_fusion
  684.2 0.6 fusion.58
  684.8 0.6 custom-call.27
  685.5 0.2 fusion.59
  685.7 0.1 fusion.61
  685.8 0.4 fusion.16
  686.2 15.6 %fusion.8 = f32[128,256,128]{2,0,1:T(8,128)} fusion(bf16[128,128,1]{1,0,2:T(8,128)(2,1)S(1)} %fusion.16, bf16[128,256,128]{2,1,0:T(8,128)(2,1)} %get-tuple-element.21), kind=kOutput, calls=%fused_computation.11 | convolution fusion | flops 1073741824 | bytes 25198592 | tf_op jit(solution)/shard_map/ij,jyx->iyx/dot_general | solution.py:98
  701.8 15.8 %fusion.10 = f32[128,256,128]{2,0,1:T(8,128)} fusion(bf16[128,128,1]{1,0,2:T(8,128)(2,1)S(1)} %fusion.15, bf16[128,256,128]{2,1,0:T(8,128)(2,1)} %get-tuple-element.22), kind=kOutput, calls=%fused_computation.13 | convolution fusion | flops 1073741824 | bytes 25198592 | tf_op jit(solution)/shard_map/ij,jyx->iyx/dot_general | solution.py:97
  717.6 31.6 %fusion.2 = bf16[128,256,128]{2,1,0:T(8,128)(2,1)} fusion(bf16[128,256,128]{2,1,0:T(8,128)(2,1)S(1)} %bitcast.129, f32[128,256,128]{2,0,1:T(8,128)} %fusion.8, f32[128,256,128]{2,0,1:T(8,128)} %fusion.10, bf16[128,256,128]{2,1,0:T(8,128)(2,1)S(1)} %bitcast.131), kind=kLoop, calls=%fused_computation.4 | loop fusion | flops 37748736 | bytes 58720256 | tf_op jit(solution)/shard_map/convert_element_type | solution.py:102
  (34 shorter events, 0.3 us)
Async XLA Ops:
  6.5 558.6 %all-reduce.3.cloned.1.call-start = ((), (), s32[]{:S(2)}) async-start(), calls=%async_computation | async-start | bytes 2097152 | tf_op jit(solution)/shard_map/psum | solution.py:91
  20.9 34.9 %copy-start = (s32[2]{0:T(128)S(1)}, s32[2]{0:T(128)}, u32[]{:S(2)}) copy-start(s32[2]{0:T(128)} %param.16) | copy-start | bytes 28
  20.9 16.3 %collective-permute-start = (bf16[128,32,128]{0,2,1:T(8,128)(2,1)S(1)}, bf16[128,32,128]{0,2,1:T(8,128)(2,1)S(1)}, u32[]{:S(2)}, u32[]{:S(2)}) collective-permute-start(bf16[128,32,128]{0,2,1:T(8,128)(2,1)S(1)} %get-tuple-element.10), channel_id=1, source_target_pairs={{0,32},{32,64},{64,96},{1,33},{33,65},{65,97},{2,34},{34,66},{66,9... | collective-permute-start | bytes 3145736 | tf_op jit(solution)/shard_map/ppermute | solution.py:20
  25.5 16.1 %collective-permute-start.1 = (bf16[128,32,128]{0,2,1:T(8,128)(2,1)S(1)}, bf16[128,32,128]{0,2,1:T(8,128)(2,1)S(1)}, u32[]{:S(2)}, u32[]{:S(2)}) collective-permute-start(bf16[128,32,128]{0,2,1:T(8,128)(2,1)S(1)} %get-tuple-element.12), channel_id=1, source_target_pairs={{32,0},{64,32},{96,64},{33,1},{65,33},{97,65},{34,2},{66,34},{98,6... | collective-permute-start | bytes 3145736 | tf_op jit(solution)/shard_map/ppermute | solution.py:22
  49.3 49.0 %collective-permute-start.2 = (bf16[128,320,32]{0,2,1:T(8,128)(2,1)}, bf16[128,320,32]{0,2,1:T(8,128)(2,1)}, u32[]{:S(2)}, u32[]{:S(2)}) collective-permute-start(bf16[128,320,32]{0,2,1:T(8,128)(2,1)} %get-tuple-element.6), channel_id=1, source_target_pairs={{0,1},{1,2},{2,3},{3,4},{4,5},{5,6},{6,7},{7,8},{8,9},{9,10},{10,1... | collective-permute-start | bytes 7864328 | tf_op jit(solution)/shard_map/ppermute | solution.py:20
  53.9 50.0 %collective-permute-start.3 = (bf16[128,320,32]{0,2,1:T(8,128)(2,1)}, bf16[128,320,32]{0,2,1:T(8,128)(2,1)}, u32[]{:S(2)}, u32[]{:S(2)}) collective-permute-start(bf16[128,320,32]{0,2,1:T(8,128)(2,1)} %get-tuple-element.8), channel_id=1, source_target_pairs={{1,0},{2,1},{3,2},{4,3},{5,4},{6,5},{7,6},{8,7},{9,8},{10,9},{11,1... | collective-permute-start | bytes 7864328 | tf_op jit(solution)/shard_map/ppermute | solution.py:22
  218.5 346.7 %copy-start.2 = (s32[8]{0:T(128)S(1)}, s32[8]{0:T(128)}, u32[]{:S(2)}) copy-start(s32[8]{0:T(128)} %param.19) | copy-start | bytes 100
  218.5 348.6 %copy-start.1 = (f32[2,128]{1,0:T(2,128)S(1)}, f32[2,128]{1,0:T(2,128)}, u32[]{:S(2)}) copy-start(f32[2,128]{1,0:T(2,128)} %param.17) | copy-start | bytes 3076
  227.9 402.7 %all-reduce.5.cloned.1.call-start = ((), (), s32[]{:S(2)}) async-start(), calls=%async_computation.1 | async-start | bytes 2097152 | tf_op jit(solution)/shard_map/psum | solution.py:91
  686.2 31.4 %slice-start = ((s8[8388608]{0:T(1024)(128)(4,1)}), s8[4194304]{0:T(1024)(128)(4,1)S(1)}, s32[]{:S(2)}) async-start(s8[8388608]{0:T(1024)(128)(4,1)} %bitcast.128), calls=%async_computation.2 | async-start | bytes 8388608
  686.2 31.4 %slice-start.2 = ((s8[8388608]{0:T(1024)(128)(4,1)}), s8[4194304]{0:T(1024)(128)(4,1)S(1)}, s32[]{:S(2)}) async-start(s8[8388608]{0:T(1024)(128)(4,1)} %bitcast.130), calls=%async_computation.4 | async-start | bytes 8388608
  701.8 15.8 %slice-start.1 = ((s8[8388608]{0:T(1024)(128)(4,1)}), s8[4194304]{0:T(1024)(128)(4,1)S(1)}, s32[]{:S(2)}) async-start(s8[8388608]{0:T(1024)(128)(4,1)} %bitcast.128), calls=%async_computation.3 | async-start | bytes 8388608
  701.8 15.8 %slice-start.3 = ((s8[8388608]{0:T(1024)(128)(4,1)}), s8[4194304]{0:T(1024)(128)(4,1)S(1)}, s32[]{:S(2)}) async-start(s8[8388608]{0:T(1024)(128)(4,1)} %bitcast.130), calls=%async_computation.5 | async-start | bytes 8388608
Sparse Core Ops, SparseCore 0:
  228.0 336.9 all-reduce.2
  567.6 62.9 all-reduce.4
